TPU v7x, 32 devices: a whole 2x2x4 slice. The times are simulated.
32 devices in a mesh: dp: 8 (over y, x, core), tensor: 4 (over z).
Axes of the slice: x: 2, y: 2, z: 4, core: 2. Of those that a mesh axis runs over, the one named last changes fastest.
Arguments:
- char_inputs: bfloat16 [131072, 256], P(('dp', 'tensor')), may hold values from -6 to 6
- char_counts: int32 [8192], P(('dp', 'tensor')), may hold values from 1 to 16
- doc_ids: int32 [8, 1024], P('dp'), may hold values from 0 to 3, never falling along the last dimension, each value on 1 to 512 neighbouring positions
- cotangent: bfloat16 [8192, 512], P('dp'), may hold values from -6 to 6
- char_norm_one: float32 [256], replicated, may hold values from 0.5 to 1.5
- char_query: bfloat16 [256, 256], replicated, may hold values from -0.375 to 0.375
- char_key: bfloat16 [256, 256], replicated, may hold values from -0.375 to 0.375
- char_value: bfloat16 [256, 256], replicated, may hold values from -0.375 to 0.375
- char_out: bfloat16 [256, 256], replicated, may hold values from -0.75 to 0.75
- char_norm_two: float32 [256], replicated, may hold values from 0.5 to 1.5
- char_up: bfloat16 [256, 1024], replicated, may hold values from -0.375 to 0.375
- char_down: bfloat16 [1024, 256], replicated, may hold values from -0.1875 to 0.1875
- char_proj: bfloat16 [256, 512], replicated, may hold values from -1.5 to 1.5
- word_norm_one: float32 [512], replicated, may hold values from 0.5 to 1.5
- word_query: bfloat16 [512, 512], P(None, 'tensor'), may hold values from -0.25 to 0.25
- word_key: bfloat16 [512, 512], P(None, 'tensor'), may hold values from -0.25 to 0.25
- word_value: bfloat16 [512, 512], P(None, 'tensor'), may hold values from -0.25 to 0.25
- word_out_proj: bfloat16 [512, 512], P('tensor'), may hold values from -1 to 1
- word_norm_two: float32 [512], replicated, may hold values from 0.5 to 1.5
- word_up: bfloat16 [512, 2048], P(None, 'tensor'), may hold values from -0.25 to 0.25
- word_down: bfloat16 [2048, 512], P('tensor'), may hold values from -0.125 to 0.125
Outputs:
- word_output: bfloat16 [8192, 512], P(('dp', 'tensor'))
- char_input_gradient: float32 [131072, 256], P(('dp', 'tensor'))
- char_norm_one_gradient: float32 [256], replicated
- char_query_gradient: float32 [256, 256], replicated
- char_key_gradient: float32 [256, 256], replicated
- char_value_gradient: float32 [256, 256], replicated
- char_out_gradient: float32 [256, 256], replicated
- char_norm_two_gradient: float32 [256], replicated
- char_up_gradient: float32 [256, 1024], replicated
- char_down_gradient: float32 [1024, 256], replicated
- char_proj_gradient: float32 [256, 512], replicated
- word_norm_one_gradient: float32 [512], replicated
- word_query_gradient: float32 [512, 512], P(None, 'tensor')
- word_key_gradient: float32 [512, 512], P(None, 'tensor')
- word_value_gradient: float32 [512, 512], P(None, 'tensor')
- word_out_proj_gradient: float32 [512, 512], P('tensor')
- word_norm_two_gradient: float32 [512], replicated
- word_up_gradient: float32 [512, 2048], P(None, 'tensor')
- word_down_gradient: float32 [2048, 512], P('tensor')
Inputs may be any that keep to these rules, and one draw needn't show every extreme that they name: Slots of a word from char_counts on are padding. `doc_ids`: ids never fall along a sequence; each document covers 1 to 512 consecutive words, one exactly that many.
All inputs are finite; a program needn't handle non-finite values.
Results may differ from a plain program's by a relative error of at most 0.018.
Values may be sent and summed in bfloat16 or wider, within the bound.
A program may use at most 192 MiB of HBM per device.

v0:
```python
import jax
import jax.numpy as jnp
from jax import lax
from jax.sharding import PartitionSpec as P

HD = 64
CHEADS = 4
CHD = 64
EPSILON = 1e-05
NEG_LARGE = -1e30


def layer_norm(values, gain_vector):
    centre = values - jnp.mean(values, axis=-1, keepdims=True)
    spread = jnp.mean(centre * centre, axis=-1, keepdims=True)
    return centre * lax.rsqrt(spread + EPSILON) * gain_vector


def gelu_tanh(values):
    return jax.nn.gelu(values, approximate=True)


def matmul(left, right):
    return jnp.dot(left, right, preferred_element_type=jnp.float32)


def contract_rows(left, right):
    return lax.dot_general(
        left, right, (((0,), (0,)), ((), ())), preferred_element_type=jnp.float32
    )


def contract_cols(left, right):
    return lax.dot_general(
        left, right, (((1,), (1,)), ((), ())), preferred_element_type=jnp.float32
    )


def block_mask(seq_docs, first_row, block_rows):
    length = seq_docs.shape[0]
    block_docs = lax.dynamic_slice_in_dim(seq_docs, first_row, block_rows, 0)
    row_ids = first_row + jnp.arange(block_rows)
    key_ids = jnp.arange(length)
    return (block_docs[:, None] == seq_docs[None, :]) & (key_ids[None, :] <= row_ids[:, None])


def attention_forward(queries, key_rows, value_rows, doc_ids, block_rows):
    length = queries.shape[1]
    score_scale = queries.shape[3] ** (-0.5)
    block_count = length // block_rows

    def sequence_pass(members):
        seq_q, seq_k, seq_v, seq_docs = members

        def block_pass(block_index):
            first_row = block_index * block_rows
            block_q = lax.dynamic_slice_in_dim(seq_q, first_row, block_rows, 0)
            allowed = block_mask(seq_docs, first_row, block_rows)
            scores = (
                jnp.einsum("qhd,khd->hqk", block_q, seq_k, preferred_element_type=jnp.float32)
                * score_scale
            )
            scores = jnp.where(allowed[None], scores, NEG_LARGE)
            row_max = jnp.max(scores, axis=-1, keepdims=True)
            exponent = jnp.exp(scores - row_max)
            row_total = jnp.sum(exponent, axis=-1, keepdims=True)
            weights_low = (exponent / row_total).astype(jnp.bfloat16)
            mixed_rows = jnp.einsum(
                "hqk,khd->qhd", weights_low, seq_v, preferred_element_type=jnp.float32
            ).astype(jnp.bfloat16)
            return (mixed_rows, (row_max + jnp.log(row_total))[..., 0])

        mixed_rows, log_totals = lax.map(block_pass, jnp.arange(block_count))
        return (mixed_rows.reshape(seq_q.shape), log_totals)

    return lax.map(sequence_pass, (queries, key_rows, value_rows, doc_ids))


def attention_backward(queries, key_rows, value_rows, doc_ids, log_totals, grad_mixed, block_rows):
    length = queries.shape[1]
    score_scale = queries.shape[3] ** (-0.5)
    block_count = length // block_rows

    def sequence_pass(members):
        seq_q, seq_k, seq_v, seq_docs, seq_logs, seq_grad = members

        def block_pass(carried, block_index):
            key_acc, value_acc = carried
            first_row = block_index * block_rows
            block_q = lax.dynamic_slice_in_dim(seq_q, first_row, block_rows, 0)
            block_grad = lax.dynamic_slice_in_dim(seq_grad, first_row, block_rows, 0)
            allowed = block_mask(seq_docs, first_row, block_rows)
            scores = (
                jnp.einsum("qhd,khd->hqk", block_q, seq_k, preferred_element_type=jnp.float32)
                * score_scale
            )
            scores = jnp.where(allowed[None], scores, NEG_LARGE)
            weights_full = jnp.exp(scores - seq_logs[block_index][..., None])
            weights_low = weights_full.astype(jnp.bfloat16)
            value_acc = value_acc + jnp.einsum(
                "hqk,qhd->khd", weights_low, block_grad, preferred_element_type=jnp.float32
            )
            grad_weights = jnp.einsum(
                "qhd,khd->hqk", block_grad, seq_v, preferred_element_type=jnp.float32
            )
            inner_sum = jnp.sum(weights_full * grad_weights, axis=-1, keepdims=True)
            grad_scores = (weights_full * (grad_weights - inner_sum)).astype(jnp.bfloat16)
            grad_block_q = (
                jnp.einsum("hqk,khd->qhd", grad_scores, seq_k, preferred_element_type=jnp.float32)
                * score_scale
            ).astype(jnp.bfloat16)
            key_acc = (
                key_acc
                + jnp.einsum(
                    "hqk,qhd->khd", grad_scores, block_q, preferred_element_type=jnp.float32
                )
                * score_scale
            )
            return ((key_acc, value_acc), grad_block_q)

        zero_rows = jnp.zeros(seq_k.shape, jnp.float32)
        (key_acc, value_acc), grad_q = lax.scan(
            block_pass, (zero_rows, zero_rows), jnp.arange(block_count)
        )
        return (
            grad_q.reshape(seq_q.shape),
            key_acc.astype(jnp.bfloat16),
            value_acc.astype(jnp.bfloat16),
        )

    return lax.map(sequence_pass, (queries, key_rows, value_rows, doc_ids, log_totals, grad_mixed))


def per_device(
    char_inputs,
    char_counts,
    doc_ids,
    cotangent,
    char_norm_one,
    char_query,
    char_key,
    char_value,
    char_out,
    char_norm_two,
    char_up,
    char_down,
    char_proj,
    word_norm_one,
    word_query,
    word_key,
    word_value,
    word_out_proj,
    word_norm_two,
    word_up,
    word_down,
):
    word_count = char_counts.shape[0]
    slot_count = char_inputs.shape[0] // word_count
    char_width = char_inputs.shape[1]
    shape_four = (word_count, slot_count, CHEADS, CHD)
    char_scale = CHD ** (-0.5)
    tensor_rank = lax.axis_index("tensor")
    base_rows = char_inputs.astype(jnp.float32)
    char_normed, pull_char_one = jax.vjp(layer_norm, base_rows, char_norm_one)
    char_normed = char_normed.astype(jnp.bfloat16)
    char_q = matmul(char_normed, char_query).astype(jnp.bfloat16).reshape(shape_four)
    char_k = matmul(char_normed, char_key).astype(jnp.bfloat16).reshape(shape_four)
    char_v = matmul(char_normed, char_value).astype(jnp.bfloat16).reshape(shape_four)
    char_scores = (
        jnp.einsum("wqhd,wkhd->whqk", char_q, char_k, preferred_element_type=jnp.float32)
        * char_scale
    )
    slot_valid = jnp.arange(slot_count)[None, :] < char_counts[:, None]
    char_scores = jnp.where(slot_valid[:, None, None, :], char_scores, NEG_LARGE)
    char_probs = jax.nn.softmax(char_scores, axis=-1)
    char_probs_low = char_probs.astype(jnp.bfloat16)
    char_mixed = jnp.einsum(
        "whqk,wkhd->wqhd", char_probs_low, char_v, preferred_element_type=jnp.float32
    )
    char_mixed = char_mixed.astype(jnp.bfloat16).reshape(word_count * slot_count, char_width)
    char_first = base_rows + matmul(char_mixed, char_out)
    char_normed_two, pull_char_two = jax.vjp(layer_norm, char_first, char_norm_two)
    char_normed_two = char_normed_two.astype(jnp.bfloat16)
    char_hidden, pull_char_gelu = jax.vjp(gelu_tanh, matmul(char_normed_two, char_up))
    char_hidden = char_hidden.astype(jnp.bfloat16)
    char_second = char_first + matmul(char_hidden, char_down)
    slot_weights = slot_valid.astype(jnp.float32) / char_counts.astype(jnp.float32)[:, None]
    pooled = jnp.sum(
        char_second.reshape(word_count, slot_count, char_width) * slot_weights[:, :, None], axis=1
    )
    pooled = pooled.astype(jnp.bfloat16)
    word_vectors = matmul(pooled, char_proj).astype(jnp.bfloat16)
    input_whole = lax.all_gather(word_vectors, "tensor", axis=0, tiled=True).astype(jnp.float32)
    normed_whole, pull_first = jax.vjp(layer_norm, input_whole, word_norm_one)
    normed = normed_whole.astype(jnp.bfloat16)
    sequences = doc_ids.shape[0]
    seq_len = doc_ids.shape[1]
    token_count = sequences * seq_len
    head_count = word_query.shape[1] // HD
    shape_heads = (sequences, seq_len, head_count, HD)
    block_rows = min(512, seq_len)
    queries = matmul(normed, word_query).astype(jnp.bfloat16).reshape(shape_heads)
    key_rows = matmul(normed, word_key).astype(jnp.bfloat16).reshape(shape_heads)
    value_rows = matmul(normed, word_value).astype(jnp.bfloat16).reshape(shape_heads)
    mixed_heads, log_totals = attention_forward(queries, key_rows, value_rows, doc_ids, block_rows)
    mixed_flat = mixed_heads.reshape(token_count, head_count * HD)
    attention_part = matmul(mixed_flat, word_out_proj)
    middle = input_whole + lax.psum(attention_part.astype(jnp.bfloat16), "tensor").astype(
        jnp.float32
    )
    normed_mid, pull_mid = jax.vjp(layer_norm, middle, word_norm_two)
    normed_mid = normed_mid.astype(jnp.bfloat16)
    hidden, pull_gelu = jax.vjp(gelu_tanh, matmul(normed_mid, word_up))
    hidden = hidden.astype(jnp.bfloat16)
    feedforward_part = matmul(hidden, word_down)
    full_output = middle + lax.psum(feedforward_part.astype(jnp.bfloat16), "tensor").astype(
        jnp.float32
    )
    word_output = lax.dynamic_slice_in_dim(full_output, tensor_rank * word_count, word_count, 0)
    word_output = word_output.astype(jnp.bfloat16)
    grad_down = contract_rows(hidden, cotangent)
    grad_pre = pull_gelu(contract_cols(cotangent, word_down))[0].astype(jnp.bfloat16)
    grad_up = contract_rows(normed_mid, grad_pre)
    mid_part = contract_cols(grad_pre, word_up)
    cotangent_full = cotangent.astype(jnp.float32)
    back_mid, grad_gain_two = pull_mid(
        lax.psum(mid_part.astype(jnp.bfloat16), "tensor").astype(jnp.float32)
    )
    grad_middle = cotangent_full + back_mid
    grad_middle_low = grad_middle.astype(jnp.bfloat16)
    grad_out_proj = contract_rows(mixed_flat, grad_middle_low)
    grad_mixed = (
        contract_cols(grad_middle_low, word_out_proj).astype(jnp.bfloat16).reshape(shape_heads)
    )
    grad_q, grad_k, grad_v = attention_backward(
        queries, key_rows, value_rows, doc_ids, log_totals, grad_mixed, block_rows
    )
    flat_shape = (token_count, head_count * HD)
    grad_q = grad_q.reshape(flat_shape)
    grad_k = grad_k.reshape(flat_shape)
    grad_v = grad_v.reshape(flat_shape)
    grad_query = contract_rows(normed, grad_q)
    grad_key = contract_rows(normed, grad_k)
    grad_value = contract_rows(normed, grad_v)
    first_part = (
        contract_cols(grad_q, word_query)
        + contract_cols(grad_k, word_key)
        + contract_cols(grad_v, word_value)
    )
    back_first, grad_gain_one = pull_first(
        lax.psum(first_part.astype(jnp.bfloat16), "tensor").astype(jnp.float32)
    )
    grad_input = lax.dynamic_slice_in_dim(
        grad_middle + back_first, tensor_rank * word_count, word_count, 0
    )
    gain_share = (tensor_rank == 0).astype(jnp.float32)
    grad_vectors = grad_input.astype(jnp.bfloat16)
    grad_proj = contract_rows(pooled, grad_vectors)
    grad_pooled = contract_cols(grad_vectors, char_proj)
    grad_second = (grad_pooled[:, None, :] * slot_weights[:, :, None]).reshape(
        word_count * slot_count, char_width
    )
    second_low = grad_second.astype(jnp.bfloat16)
    grad_char_down = contract_rows(char_hidden, second_low)
    grad_char_pre = pull_char_gelu(contract_cols(second_low, char_down))[0].astype(jnp.bfloat16)
    grad_char_up = contract_rows(char_normed_two, grad_char_pre)
    back_char_two, grad_char_gain_two = pull_char_two(contract_cols(grad_char_pre, char_up))
    grad_first = grad_second + back_char_two
    first_low = grad_first.astype(jnp.bfloat16)
    grad_char_out = contract_rows(char_mixed, first_low)
    grad_char_mixed = contract_cols(first_low, char_out).astype(jnp.bfloat16).reshape(shape_four)
    grad_char_probs = jnp.einsum(
        "wqhd,wkhd->whqk", grad_char_mixed, char_v, preferred_element_type=jnp.float32
    )
    char_inner = jnp.sum(char_probs * grad_char_probs, axis=-1, keepdims=True)
    grad_char_scores = (char_probs * (grad_char_probs - char_inner)).astype(jnp.bfloat16)
    flat_chars = (word_count * slot_count, char_width)
    grad_cv = jnp.einsum(
        "whqk,wqhd->wkhd", char_probs_low, grad_char_mixed, preferred_element_type=jnp.float32
    )
    grad_cv = grad_cv.astype(jnp.bfloat16).reshape(flat_chars)
    grad_cq = jnp.einsum(
        "whqk,wkhd->wqhd", grad_char_scores, char_k, preferred_element_type=jnp.float32
    )
    grad_cq = (grad_cq * char_scale).astype(jnp.bfloat16).reshape(flat_chars)
    grad_ck = jnp.einsum(
        "whqk,wqhd->wkhd", grad_char_scores, char_q, preferred_element_type=jnp.float32
    )
    grad_ck = (grad_ck * char_scale).astype(jnp.bfloat16).reshape(flat_chars)
    grad_char_query = contract_rows(char_normed, grad_cq)
    grad_char_key = contract_rows(char_normed, grad_ck)
    grad_char_value = contract_rows(char_normed, grad_cv)
    back_char_one, grad_char_gain_one = pull_char_one(
        contract_cols(grad_cq, char_query)
        + contract_cols(grad_ck, char_key)
        + contract_cols(grad_cv, char_value)
    )
    char_input_gradient = grad_first + back_char_one
    word_sums = lax.psum(
        (grad_query, grad_key, grad_value, grad_out_proj, grad_up, grad_down), "dp"
    )
    char_sums = lax.psum(
        (
            grad_char_gain_one,
            grad_char_query,
            grad_char_key,
            grad_char_value,
            grad_char_out,
            grad_char_gain_two,
            grad_char_up,
            grad_char_down,
            grad_proj,
            grad_gain_one * gain_share,
            grad_gain_two * gain_share,
        ),
        ("dp", "tensor"),
    )
    return (
        word_output,
        char_input_gradient,
        char_sums[0],
        char_sums[1],
        char_sums[2],
        char_sums[3],
        char_sums[4],
        char_sums[5],
        char_sums[6],
        char_sums[7],
        char_sums[8],
        char_sums[9],
        word_sums[0],
        word_sums[1],
        word_sums[2],
        word_sums[3],
        char_sums[10],
        word_sums[4],
        word_sums[5],
    )


def solution(mesh):
    in_specs = (
        P(("dp", "tensor"), None),
        P(("dp", "tensor")),
        P("dp", None),
        P("dp", None),
        P(),
        P(),
        P(),
        P(),
        P(),
        P(),
        P(),
        P(),
        P(),
        P(),
        P(None, "tensor"),
        P(None, "tensor"),
        P(None, "tensor"),
        P("tensor", None),
        P(),
        P(None, "tensor"),
        P("tensor", None),
    )
    out_specs = (
        P(("dp", "tensor"), None),
        P(("dp", "tensor"), None),
        P(),
        P(),
        P(),
        P(),
        P(),
        P(),
        P(),
        P(),
        P(),
        P(),
        P(None, "tensor"),
        P(None, "tensor"),
        P(None, "tensor"),
        P("tensor", None),
        P(),
        P(None, "tensor"),
        P("tensor", None),
    )
    return jax.shard_map(
        per_device, mesh=mesh, in_specs=in_specs, out_specs=out_specs, check_vma=False
    )
```

profile of v0, /device:TPU:0, one launch (start us, length us, event | category | flops | bytes accessed | tf_op | source)
XLA Modules:
  0.0 727.3 jit_solution(17585414568510393199)
XLA Ops:
  20.2 7.1 reshape.407
  30.9 7.1 reshape.406
  41.6 7.1 reshape.405
  48.7 5.8 fusion.75
  54.5 28.7 %fusion.134 = (f32[256,4,16]{2,1,0:T(4,128)S(1)}, f32[256,4,16,16]{2,3,1,0:T(8,128)S(1)}) fusion(f32[256,4,16,16]{2,3,1,0:T(8,128)S(1)} %fusion.75, pred[256,16]{1,0:T(8,128)(4,1)S(1)} %iota_compare_fusion.2), kind=kOutput, calls=%fused_computation.213 | output fusion | flops 1572879 | bytes 2166784 | tf_op jit(solution)/shard_map/sub | solution.py:175
  94.6 7.0 reshape.408
  106.1 9.7 %multiply_convert_fusion.1 = (bf16[4096,1024]{1,0:T(8,128)(2,1)S(1)}, f32[4096,1024]{1,0:T(8,128)}) fusion(bf16[256,1024]{1,0:T(8,128)(2,1)S(1)} %copy-done, f32[4096,256]{1,0:T(8,128)S(1)} %get-tuple-element.291, f32[256]{0:T(256)S(1)} %copy-done.97, f32[4096]{0:T(1024)S(1)} %fusion.121, f32[4096]{0:T(1024)S(1)} %broadcast_multiply_fusion), kind=kOutput, calls=%fused_computation.59 | convolution fusion | flops 2189426688 | bytes 29918208 | tf_op jit(solution)/shard_map/dot_general | solution.py:24
  120.1 30.8 %all-gather.2.cloned.1.call-done = bf16[1024,512]{1,0:T(8,128)(2,1)} async-done(((bf16[256,512]{1,0:T(8,128)(2,1)}), bf16[1024,512]{1,0:T(8,128)(2,1)}) %all-gather.2.cloned.1.call-update) | async-done | bytes 1048592 | tf_op jit(solution)/shard_map/all_gather | solution.py:193
  158.7 16.5 %while.47 = (s32[]{:T(128)}, bf16[2,512,2,64]{1,3,2,0:T(8,128)(2,1)S(1)}, f32[2,2,512]{2,1,0:T(2,128)}, s32[2]{0:T(128)S(1)}, s32[1024]{0:T(1024)S(1)}, /*index=...) while((s32[]{:T(128)}, ...), condition=%wide.region_12.13_spmd, body=%wide.region_9.12_spmd.sunk | while | flops 282656256 | bytes 15513803 | solution.py:73
  182.1 47.9 %all-reduce.10.cloned.1.call-done = bf16[1024,512]{1,0:T(8,128)(2,1)} async-done(((bf16[1024,512]{1,0:T(8,128)(2,1)}), bf16[1024,512]{1,0:T(8,128)(2,1)}) %all-reduce.10.cloned.1.call-update) | async-done | bytes 1048592 | tf_op jit(solution)/shard_map/psum | solution.py:208
  243.4 47.8 %all-reduce.12.cloned.1.call-done = bf16[1024,512]{1,0:T(8,128)(2,1)} async-done(((bf16[1024,512]{1,0:T(8,128)(2,1)}), bf16[1024,512]{1,0:T(8,128)(2,1)}) %all-reduce.12.cloned.1.call-update) | async-done | bytes 1048592 | tf_op jit(solution)/shard_map/psum | solution.py:227
  302.9 28.6 %while.48 = (s32[]{:T(128)}, f32[1024,2,64]{0,2,1:T(8,128)S(1)}, f32[1024,2,64]{0,2,1:T(8,128)}, bf16[2,512,2,64]{1,3,2,0:T(8,128)(2,1)}, s32[2]{0:T(128)S(1)}, ...) while((s32[]{:T(128)}, f32[1024,2,64]{0,2,1:T(8,128)S(1)}, ...), condition=%wide.region_22.23_spmd.clone, body=%wide.region_20.22_spmd.clone.sunk | while | flops 689176064 | bytes 44476844 | solution.py:122
  347.7 75.2 %all-reduce.18.cloned.1.call-done = (bf16[1024,512]{1,0:T(8,128)(2,1)}, bf16[1024,512]{1,0:T(8,128)(2,1)}) async-done(((bf16[1024,512]{1,0:T(8,128)(2,1)}, bf16[1024,512]{1,0:T(8,128)(2,1)}), (bf16[1024,512]{1,0:T(8,128)(2,1)}, bf16[1024,512]{1,0:T(8,128)(2,1)})) %all-reduce.18.cloned.1.call-update) | async-done | bytes 2097168 | tf_op jit(solution)/shard_map/psum | solution.py:216
  431.6 15.4 %fusion.47 = bf16[4096,1024]{1,0:T(8,128)(2,1)S(1)} fusion(f32[4096,1024]{1,0:T(8,128)} %get-tuple-element.293, bf16[4096,256]{1,0:T(8,128)(2,1)S(1)} %fusion.62, bf16[1024,256]{1,0:T(8,128)(2,1)S(1)} %copy-done.54), kind=kOutput, calls=%fused_computation.58 | convolution fusion | flops 2231369728 | bytes 27787264 | tf_op jit(solution)/shard_map/dot_general | solution.py:34
  462.3 9.0 %convert_bitcast_fusion = bf16[256,16,4,64]{3,1,2,0:T(8,128)(2,1)} fusion(bf16[256,16,4,64]{3,2,1,0:T(4,128)(2,1)} %reshape.414, f32[256,4,16,16]{2,3,1,0:T(8,128)} %copy-done.21, f32[256,4,16]{2,1,0:T(4,128)S(1)} %copy-done.56), kind=kOutput, calls=%fused_computation.96 | convolution fusion | flops 35127296 | bytes 5308416 | tf_op jit(solution)/shard_map/whqk,wqhd->wkhd/dot_general | solution.py:278
  471.4 12.3 %multiply_reduce_fusion.1 = (f32[256,4,16]{2,1,0:T(4,128)S(1)}, f32[256,4,16,16]{2,3,1,0:T(8,128)}) fusion(f32[256,4,16,16]{2,3,1,0:T(8,128)} %copy-done.21, f32[256,4,16]{2,1,0:T(4,128)S(1)} %copy-done.56, bf16[256,16,4,64]{3,2,1,0:T(4,128)(2,1)} %reshape.405, bf16[256,16,4,64]{3,2,1,0:T(4,128)(2,1)} %reshape.414), kind=kOutput, calls=%fused_computation.63 | convolution fusion | flops 34324480 | bytes 6422528 | tf_op jit(solution)/shard_map/wqhd,wkhd->whqk/dot_general | solution.py:272
  483.7 7.6 %multiply_convert_fusion.4 = bf16[256,4,16,16]{2,3,1,0:T(8,128)(2,1)S(1)} fusion(f32[256,4,16,16]{2,3,1,0:T(8,128)} %get-tuple-element.298, f32[256,4,16]{2,1,0:T(4,128)S(1)} %get-tuple-element.297, f32[256,4,16,16]{2,3,1,0:T(8,128)} %copy-done.21, f32[256,4,16]{2,1,0:T(4,128)S(1)} %copy-done.56), kind=kLoop, calls=%fused_computation.62 | loop fusion | flops 1048576 | bytes 2752512 | tf_op jit(solution)/shard_map/convert_element_type | solution.py:276
  502.2 7.1 reshape.415
  520.1 7.0 reshape.417
  534.5 7.1 reshape.416
  553.9 7.5 %fusion.130 = f32[256,1024]{1,0:T(8,128)} fusion(bf16[4096,1024]{1,0:T(8,128)(2,1)} %copy-done.101, f32[4096,256]{1,0:T(8,128)S(1)} %copy-done.8, f32[256]{0:T(256)S(1)} %copy-done.98, f32[4096]{0:T(1024)S(1)} %copy-done.83, f32[4096]{0:T(1024)S(1)} %copy-done.75), kind=kOutput, calls=%fused_computation.209 | convolution fusion | flops 2151677952 | bytes 13665280 | tf_op jit(solution)/shard_map/dot_general | solution.py:28
  570.4 5.9 add_add_fusion.2
  576.2 40.0 %all-reduce = (f32[256]{0:T(256)}, f32[256]{0:T(256)}, f32[512]{0:T(512)}, f32[512]{0:T(512)}) all-reduce(f32[256]{0:T(256)S(1)} %get-tuple-element.215, f32[256]{0:T(256)S(1)} %get-tuple-element.213, f32[512]{0:T(512)S(1)} %get-tuple-element.302, f32[512]{0:T(512)S(1)} %get-tuple-element.301), channel_id=1, replica_groups=mesh['dp'=8,'tensor'=4] {'dp','tensor'}, use_global_device_ids=true, to_apply=%region_32.33 | all-reduce | flops 1536 | bytes 12288 | tf_op jit(solution)/shard_map/psum | solution.py:302
  618.2 86.3 %all-reduce.14.cloned.1.call-done = (f32[256,256]{1,0:T(8,128)}, f32[256,256]{1,0:T(8,128)}, f32[256,256]{1,0:T(8,128)}, f32[256,256]{1,0:T(8,128)}, f32[256,102...) async-done(((f32[256,256]{1,0:T(8,128)}, f32[256,256]{1,0:T(8,128)}, f32[256,256]{1,0:T(8,128)}, f32[256,256]{1,0:T(8,128)}, f32[256,1024]{1,0:T(8,128)}, ...) | async-done | bytes 3670032 | tf_op jit(solution)/shard_map/psum | solution.py:302
  (385 shorter events, 225.4 us)
Async XLA Ops:
  7.2 98.9 %copy-start = (bf16[256,1024]{1,0:T(8,128)(2,1)S(1)}, bf16[256,1024]{1,0:T(8,128)(2,1)}, u32[]{:S(2)}) copy-start(bf16[256,1024]{1,0:T(8,128)(2,1)} %param.35) | copy-start | bytes 1572868
  7.2 143.7 %all-gather.2.cloned.1.call-start = ((), (), s32[]{:S(2)}) async-start(), calls=%async_computation | async-start | bytes 1310720 | tf_op jit(solution)/shard_map/all_gather | solution.py:193
  14.5 101.3 %copy-start.34 = (f32[256,16]{1,0:T(8,128)}, f32[256,16]{1,0:T(8,128)S(1)}, u32[]{:S(2)}) copy-start(f32[256,16]{1,0:T(8,128)S(1)} %convert_divide_fusion) | copy-start | bytes 49156
  115.8 38.3 %copy-start.90 = (f32[512]{0:T(512)S(1)}, f32[512]{0:T(512)}, u32[]{:S(2)}) copy-start(f32[512]{0:T(512)} %param.38) | copy-start | bytes 6148
  119.1 36.7 %copy-start.66 = (bf16[512,128]{1,0:T(8,128)(2,1)S(1)}, bf16[512,128]{1,0:T(8,128)(2,1)}, u32[]{:S(2)}) copy-start(bf16[512,128]{1,0:T(8,128)(2,1)} %param.41) | copy-start | bytes 393220
  119.1 37.9 %copy-start.63 = (bf16[512,128]{1,0:T(8,128)(2,1)S(1)}, bf16[512,128]{1,0:T(8,128)(2,1)}, u32[]{:S(2)}) copy-start(bf16[512,128]{1,0:T(8,128)(2,1)} %param.40) | copy-start | bytes 393220
  119.1 38.3 %copy-start.64 = (bf16[512,128]{1,0:T(8,128)(2,1)S(1)}, bf16[512,128]{1,0:T(8,128)(2,1)}, u32[]{:S(2)}) copy-start(bf16[512,128]{1,0:T(8,128)(2,1)} %param.39) | copy-start | bytes 393220
  120.0 109.9 %all-reduce.10.cloned.1.call-start = ((), (), s32[]{:S(2)}) async-start(), calls=%async_computation.1 | async-start | bytes 2097152 | tf_op jit(solution)/shard_map/psum | solution.py:208
  120.1 38.5 %copy-start.44 = (s32[1,1024]{1,0:T(1,128)S(1)}, s32[1,1024]{1,0:T(1,128)}, u32[]{:S(2)}) copy-start(s32[1,1024]{1,0:T(1,128)} %param.27) | copy-start | bytes 12292
  175.2 54.8 %copy-start.1 = (bf16[1024,512]{1,0:T(8,128)(2,1)S(1)}, bf16[1024,512]{1,0:T(8,128)(2,1)}, u32[]{:S(2)}) copy-start(bf16[1024,512]{1,0:T(8,128)(2,1)} %all-gather.2.cloned.1.call-done) | copy-start | bytes 3145732
  178.6 54.9 %copy-start.88 = (f32[512]{0:T(512)S(1)}, f32[512]{0:T(512)}, u32[]{:S(2)}) copy-start(f32[512]{0:T(512)} %param.43) | copy-start | bytes 6148
  178.6 112.5 %all-reduce.12.cloned.1.call-start = ((), (), s32[]{:S(2)}) async-start(), calls=%async_computation.2 | async-start | bytes 2097152 | tf_op jit(solution)/shard_map/psum | solution.py:227
  239.8 183.1 %all-reduce.18.cloned.1.call-start = ((), (), s32[]{:S(2)}) async-start(), calls=%async_computation.5 | async-start | bytes 4194304 | tf_op jit(solution)/shard_map/psum | solution.py:216
  337.3 280.8 %all-reduce.16.cloned.1.call-start = ((), (), s32[]{:S(2)}) async-start(), calls=%async_computation.4 | async-start | bytes 6291456 | tf_op jit(solution)/shard_map/psum | solution.py:299
  344.0 78.9 %copy-start.81 = (f32[1024]{0:T(1024)S(1)}, f32[1024]{0:T(1024)}, u32[]{:S(2)}) copy-start(f32[1024]{0:T(1024)} %copy-done.80) | copy-start | bytes 12292
  344.1 78.9 %copy-start.85 = (f32[1024]{0:T(1024)S(1)}, f32[1024]{0:T(1024)}, u32[]{:S(2)}) copy-start(f32[1024]{0:T(1024)} %copy-done.84) | copy-start | bytes 12292
  344.1 78.9 %copy-start.91 = (f32[512]{0:T(512)S(1)}, f32[512]{0:T(512)}, u32[]{:S(2)}) copy-start(f32[512]{0:T(512)} %param.38) | copy-start | bytes 6148
  346.4 79.6 %copy-start.87 = (f32[1024]{0:T(1024)S(1)}, f32[1024]{0:T(1024)}, u32[]{:S(2)}) copy-start(f32[1024]{0:T(1024)} %copy-done.86) | copy-start | bytes 12292
  347.5 82.1 %copy-start.37 = (bf16[256,512]{1,0:T(8,128)(2,1)S(1)}, bf16[256,512]{1,0:T(8,128)(2,1)}, u32[]{:S(2)}) copy-start(bf16[256,512]{1,0:T(8,128)(2,1)} %param.37) | copy-start | bytes 786436
  347.5 356.9 %all-reduce.14.cloned.1.call-start = ((), (), s32[]{:S(2)}) async-start(), calls=%async_computation.3 | async-start | bytes 7340032 | tf_op jit(solution)/shard_map/psum | solution.py:302
  431.5 15.5 %copy-start.23 = (bf16[4096,256]{1,0:T(8,128)(2,1)}, bf16[4096,256]{1,0:T(8,128)(2,1)S(1)}, u32[]{:S(2)}) copy-start(bf16[4096,256]{1,0:T(8,128)(2,1)S(1)} %fusion.62) | copy-start | bytes 6291460
  431.6 15.5 %copy-start.7 = (f32[4096,256]{1,0:T(8,128)S(1)}, f32[4096,256]{1,0:T(8,128)}, u32[]{:S(2)}) copy-start(f32[4096,256]{1,0:T(8,128)} %copy-done.6) | copy-start | bytes 12582916
  618.2 97.4 %copy-start.71 = (f32[512,128]{1,0:T(8,128)S(1)}, f32[512,128]{1,0:T(8,128)}, u32[]{:S(2)}) copy-start(f32[512,128]{1,0:T(8,128)} %get-tuple-element.523) | copy-start | bytes 786436
  618.2 98.1 %copy-start.70 = (f32[512,128]{1,0:T(8,128)S(1)}, f32[512,128]{1,0:T(8,128)}, u32[]{:S(2)}) copy-start(f32[512,128]{1,0:T(8,128)} %get-tuple-element.524) | copy-start | bytes 786436
  (92 other events, 477.6 us)
Sparse Core Ops, SparseCore 0:
  120.2 30.6 all-gather.1
  178.7 51.2 all-reduce.9
  239.9 51.1 all-reduce.11
  337.5 85.4 all-reduce.17
  427.9 69.0 all-reduce.15
  561.6 142.8 all-reduce.13
where the time goes:
time: 738 us; the launch traced here: 727 us
  waiting for transfers between devices  288 us (39%)
  matrix products  176 us (24%)
  local copies, waits for them, and re-layouts  106 us (14%)
  other arithmetic  94.6 us (13%)
  blocking collectives  40 us (5%)
  between operations  15.6 us (2%)
    psum x1, waiting for transfers between devices, per_device(): lax.psum((grad_char_gain_one, grad_char_query, grad_char_key, grad_char_v...  86.3 us
    psum x1, waiting for transfers between devices, per_device(): lax.psum(feedforward_part.astype(jnp.bfloat16), 'tensor')  75.2 us
    psum x1, waiting for transfers between devices, per_device(): lax.psum(attention_part.astype(jnp.bfloat16), 'tensor').astype(jnp.float32)  47.9 us
    psum x1, waiting for transfers between devices, per_device(): lax.psum(mid_part.astype(jnp.bfloat16), 'tensor').astype(jnp.float32)  47.8 us
    dot_general x13, matrix products, contract_cols(): lax.dot_general(left, right, (((1,), (1,)), ((), ())), preferred_element_...  43 us
    psum x1, blocking collectives, per_device(): lax.psum((grad_char_gain_one, grad_char_query, grad_char_key, grad_char_v...  40 us
    dot_general x13, matrix products, matmul(): return jnp.dot(left, right, preferred_element_type=jnp.float32)  37.2 us
    dot_general x13, matrix products, contract_rows(): lax.dot_general(left, right, (((0,), (0,)), ((), ())), preferred_element_...  32.8 us
  transfers between devices with their start and end apart: 6, of which 5 were waited for; matrix products, arithmetic and copies ran while one was open for 23% of the time, Pallas kernels for 0%

commit v1 on v0

--- a/solution.py
+++ b/solution.py
@@ -8,6 +8,28 @@
 CHD = 64
 EPSILON = 1e-05
 NEG_LARGE = -1e30
+
+
+def joined_along(blocks, dim):
+    dims = list(blocks.shape[1:])
+    dims[dim] *= blocks.shape[0]
+    return jnp.moveaxis(blocks, 0, dim).reshape(dims)
+
+
+def gather_around(x, axis, dim):
+    count = lax.axis_size(axis)
+    pairs = [(i, (i + 1) % count) for i in range(count)]
+    back = [(b, a) for a, b in pairs]
+    lower, upper = ([], [])
+    for hop in range(count - 1):
+        if hop % 2 == 0:
+            lower.append(lax.ppermute(lower[-1] if lower else x, axis, pairs))
+        else:
+            upper.append(lax.ppermute(upper[-1] if upper else x, axis, back))
+    tiles = jnp.stack([*lower[::-1], x, *upper])
+    shift = lax.axis_index(axis) - len(lower)
+    tiles = tiles[(jnp.arange(count) - shift) % count]
+    return joined_along(tiles, dim)
 
 
 def layer_norm(values, gain_vector):
@@ -190,7 +212,7 @@
     )
     pooled = pooled.astype(jnp.bfloat16)
     word_vectors = matmul(pooled, char_proj).astype(jnp.bfloat16)
-    input_whole = lax.all_gather(word_vectors, "tensor", axis=0, tiled=True).astype(jnp.float32)
+    input_whole = gather_around(word_vectors, "tensor", 0).astype(jnp.float32)
     normed_whole, pull_first = jax.vjp(layer_norm, input_whole, word_norm_one)
     normed = normed_whole.astype(jnp.bfloat16)
     sequences = doc_ids.shape[0]

time: 738 us -> 716 us (0.970)
  waiting for transfers between devices: 288 us -> 274 us
  matrix products: 176 us -> 168 us
    all_gather x1 -> x0, waiting for transfers between devices: 30.8 us -> none  [per_device(): lax.all_gather(word_vectors, 'tensor', axis=0, tiled=True)]
    ppermute x0 -> x3, waiting for transfers between devices: none -> 17.5 us  [the longest x2 13.2 us: gather_around(): lower.append(lax.ppermute(lower[-1] if lower else x, axis, pairs))]
    unnamed x215 -> x223, local copies, waits for them, and re-layouts: 29.2 us -> 27.6 us
  transfers between devices with their start and end apart: 6 -> 8, of which waited for: 5 -> 7; matrix products, arithmetic and copies ran while one was open for 23% -> 24% of each run, Pallas kernels for 0% -> 0%
where the time goes in v1:
time: 716 us; the launch traced here: 705 us
  waiting for transfers between devices  274 us (38%)
  matrix products  168 us (23%)
  local copies, waits for them, and re-layouts  103 us (14%)
  other arithmetic  92 us (13%)
  blocking collectives  40 us (6%)
  between operations  15.4 us (2%)
    psum x1, waiting for transfers between devices, per_device(): lax.psum((grad_char_gain_one, grad_char_query, grad_char_key, grad_char_v...  86.3 us
    psum x1, waiting for transfers between devices, per_device(): lax.psum(feedforward_part.astype(jnp.bfloat16), 'tensor')  74.6 us
    psum x1, waiting for transfers between devices, per_device(): lax.psum(attention_part.astype(jnp.bfloat16), 'tensor').astype(jnp.float32)  48.2 us
    psum x1, waiting for transfers between devices, per_device(): lax.psum(mid_part.astype(jnp.bfloat16), 'tensor').astype(jnp.float32)  47.8 us
    dot_general x13, matrix products, contract_cols(): lax.dot_general(left, right, (((1,), (1,)), ((), ())), preferred_element_...  41 us
    psum x1, blocking collectives, per_device(): lax.psum((grad_char_gain_one, grad_char_query, grad_char_key, grad_char_v...  40 us
    dot_general x13, matrix products, matmul(): return jnp.dot(left, right, preferred_element_type=jnp.float32)  36.6 us
    dot_general x13, matrix products, contract_rows(): lax.dot_general(left, right, (((0,), (0,)), ((), ())), preferred_element_...  34.2 us
  transfers between devices with their start and end apart: 8, of which 7 were waited for; matrix products, arithmetic and copies ran while one was open for 24% of the time, Pallas kernels for 0%

profile of v1, /device:TPU:0, one launch (start us, length us, event | category | flops | bytes accessed | tf_op | source)
XLA Modules:
  0.0 705.2 jit_solution(2421125756293345555)
XLA Ops:
  20.8 7.1 %reshape.667 = bf16[256,16,4,64]{3,2,1,0:T(4,128)(2,1)} reshape(bf16[4096,256]{1,0:T(8,128)(2,1)} %convolution_convert_fusion.1) | data formatting | bytes 4194304 | tf_op jit(solution)/shard_map/reshape | solution.py:189
  31.5 7.1 %reshape.666 = bf16[256,16,4,64]{3,2,1,0:T(4,128)(2,1)} reshape(bf16[4096,256]{1,0:T(8,128)(2,1)} %convolution_convert_fusion.2) | data formatting | bytes 4194304 | tf_op jit(solution)/shard_map/reshape | solution.py:188
  42.2 7.1 %reshape.665 = bf16[256,16,4,64]{3,2,1,0:T(4,128)(2,1)} reshape(bf16[4096,256]{1,0:T(8,128)(2,1)} %convolution_convert_fusion.3) | data formatting | bytes 4194304 | tf_op jit(solution)/shard_map/reshape | solution.py:190
  55.1 28.7 %fusion.141 = (f32[256,4,16]{2,1,0:T(4,128)S(1)}, f32[256,4,16,16]{2,3,1,0:T(8,128)S(1)}) fusion(f32[256,4,16,16]{2,3,1,0:T(8,128)S(1)} %fusion.75, pred[256,16]{1,0:T(8,128)(4,1)S(1)} %iota_compare_fusion.2), kind=kOutput, calls=%fused_computation.228 | output fusion | flops 1572879 | bytes 2166784 | tf_op jit(solution)/shard_map/sub | solution.py:197
  95.2 7.0 reshape.668
  106.7 9.7 %multiply_convert_fusion.1 = (bf16[4096,1024]{1,0:T(8,128)(2,1)S(1)}, f32[4096,1024]{1,0:T(8,128)}) fusion(bf16[256,1024]{1,0:T(8,128)(2,1)S(1)} %copy-done, f32[4096,256]{1,0:T(8,128)S(1)} %get-tuple-element.295, f32[256]{0:T(256)S(1)} %copy-done.99, f32[4096]{0:T(1024)S(1)} %fusion.124, f32[4096]{0:T(1024)S(1)} %broadcast_multiply_fusion), kind=kOutput, calls=%fused_computation.60 | convolution fusion | flops 2189426688 | bytes 29918208 | tf_op jit(solution)/shard_map/dot_general | solution.py:46
  125.1 7.1 %collective-permute-done = bf16[256,512]{1,0:T(8,128)(2,1)S(1)} collective-permute-done((bf16[256,512]{1,0:T(8,128)(2,1)S(1)}, bf16[256,512]{1,0:T(8,128)(2,1)S(1)}, u32[]{:S(2)}, u32[]{:S(2)}) %collective-permute-start) | collective-permute-done | bytes 262176 | tf_op jit(solution)/shard_map/ppermute | solution.py:26
  136.5 6.1 collective-permute-done.1
  147.7 12.8 %while.47 = (s32[]{:T(128)}, bf16[2,512,2,64]{1,3,2,0:T(8,128)(2,1)}, f32[2,2,512]{2,1,0:T(2,128)S(1)}, s32[2]{0:T(128)S(1)}, s32[1024]{0:T(1024)S(1)}, /*index=...) while((s32[]{:T(128)}, ...), condition=%wide.region_12.13_spmd, body=%wide.region_9.12_spmd.sunk | while | flops 282656256 | bytes 15513803 | solution.py:95
  168.2 48.2 %all-reduce.10.cloned.1.call-done = bf16[1024,512]{1,0:T(8,128)(2,1)} async-done(((bf16[1024,512]{1,0:T(8,128)(2,1)}), bf16[1024,512]{1,0:T(8,128)(2,1)}) %all-reduce.10.cloned.1.call-update) | async-done | bytes 1048592 | tf_op jit(solution)/shard_map/psum | solution.py:230
  230.5 47.8 %all-reduce.12.cloned.1.call-done = bf16[1024,512]{1,0:T(8,128)(2,1)} async-done(((bf16[1024,512]{1,0:T(8,128)(2,1)}), bf16[1024,512]{1,0:T(8,128)(2,1)}) %all-reduce.12.cloned.1.call-update) | async-done | bytes 1048592 | tf_op jit(solution)/shard_map/psum | solution.py:249
  288.0 24.3 %while.48 = (s32[]{:T(128)}, f32[1024,2,64]{0,2,1:T(8,128)S(1)}, f32[1024,2,64]{0,2,1:T(8,128)}, bf16[2,512,2,64]{1,3,2,0:T(8,128)(2,1)S(1)}, s32[2]{0:T(128)S(1...) while((s32[]{:T(128)}, f32[1024,2,64]{0,2,1:T(8,128)S(1)}, ...), condition=%wide.region_22.23_spmd.clone, body=%wide.region_20.22_spmd.clone.sunk | while | flops 689176064 | bytes 43428240 | solution.py:144
  327.4 74.6 %all-reduce.18.cloned.1.call-done = (bf16[1024,512]{1,0:T(8,128)(2,1)}, bf16[1024,512]{1,0:T(8,128)(2,1)}) async-done(((bf16[1024,512]{1,0:T(8,128)(2,1)}, bf16[1024,512]{1,0:T(8,128)(2,1)}), (bf16[1024,512]{1,0:T(8,128)(2,1)}, bf16[1024,512]{1,0:T(8,128)(2,1)})) %all-reduce.18.cloned.1.call-update) | async-done | bytes 2097168 | tf_op jit(solution)/shard_map/psum | solution.py:238
  410.7 15.4 %fusion.47 = bf16[4096,1024]{1,0:T(8,128)(2,1)S(1)} fusion(f32[4096,1024]{1,0:T(8,128)} %get-tuple-element.297, bf16[4096,256]{1,0:T(8,128)(2,1)S(1)} %fusion.62, bf16[1024,256]{1,0:T(8,128)(2,1)S(1)} %copy-done.52), kind=kOutput, calls=%fused_computation.59 | convolution fusion | flops 2231369728 | bytes 27787264 | tf_op jit(solution)/shard_map/dot_general | solution.py:56
  441.4 9.0 %convert_bitcast_fusion = bf16[256,16,4,64]{3,1,2,0:T(8,128)(2,1)} fusion(bf16[256,16,4,64]{3,2,1,0:T(4,128)(2,1)} %reshape.674, f32[256,4,16,16]{2,3,1,0:T(8,128)} %copy-done.21, f32[256,4,16]{2,1,0:T(4,128)S(1)} %copy-done.54), kind=kOutput, calls=%fused_computation.97 | convolution fusion | flops 35127296 | bytes 5308416 | tf_op jit(solution)/shard_map/whqk,wqhd->wkhd/dot_general | solution.py:300
  450.4 12.3 %multiply_reduce_fusion.1 = (f32[256,4,16]{2,1,0:T(4,128)S(1)}, f32[256,4,16,16]{2,3,1,0:T(8,128)}) fusion(f32[256,4,16,16]{2,3,1,0:T(8,128)} %copy-done.21, f32[256,4,16]{2,1,0:T(4,128)S(1)} %copy-done.54, bf16[256,16,4,64]{3,2,1,0:T(4,128)(2,1)} %reshape.665, bf16[256,16,4,64]{3,2,1,0:T(4,128)(2,1)} %reshape.674), kind=kOutput, calls=%fused_computation.64 | convolution fusion | flops 34324480 | bytes 6422528 | tf_op jit(solution)/shard_map/wqhd,wkhd->whqk/dot_general | solution.py:294
  462.7 7.6 %multiply_convert_fusion.4 = bf16[256,4,16,16]{2,3,1,0:T(8,128)(2,1)S(1)} fusion(f32[256,4,16,16]{2,3,1,0:T(8,128)} %get-tuple-element.302, f32[256,4,16]{2,1,0:T(4,128)S(1)} %get-tuple-element.301, f32[256,4,16,16]{2,3,1,0:T(8,128)} %copy-done.21, f32[256,4,16]{2,1,0:T(4,128)S(1)} %copy-done.54), kind=kLoop, calls=%fused_computation.63 | loop fusion | flops 1048576 | bytes 2752512 | tf_op jit(solution)/shard_map/convert_element_type | solution.py:298
  481.3 6.0 reshape.675
  497.9 6.0 reshape.677
  512.0 7.1 %reshape.676 = bf16[4096,256]{1,0:T(8,128)(2,1)} reshape(bf16[256,16,4,64]{3,2,1,0:T(4,128)(2,1)} %copy.69) | data formatting | bytes 4194304 | tf_op jit(solution)/shard_map/reshape | solution.py:311
  532.1 7.5 %fusion.137 = f32[256,1024]{1,0:T(8,128)} fusion(bf16[4096,1024]{1,0:T(8,128)(2,1)} %copy-done.103, f32[4096,256]{1,0:T(8,128)S(1)} %copy-done.5, f32[256]{0:T(256)S(1)} %copy-done.100, f32[4096]{0:T(1024)S(1)} %copy-done.80, f32[4096]{0:T(1024)S(1)} %copy-done.74), kind=kOutput, calls=%fused_computation.224 | convolution fusion | flops 2151677952 | bytes 13665280 | tf_op jit(solution)/shard_map/dot_general | solution.py:50
  548.5 5.9 add_add_fusion.2
  554.4 40.0 %all-reduce = (f32[256]{0:T(256)}, f32[256]{0:T(256)}, f32[512]{0:T(512)}, f32[512]{0:T(512)}) all-reduce(f32[256]{0:T(256)S(1)} %get-tuple-element.215, f32[256]{0:T(256)S(1)} %get-tuple-element.213, f32[512]{0:T(512)S(1)} %get-tuple-element.306, f32[512]{0:T(512)S(1)} %get-tuple-element.305), channel_id=1, replica_groups=mesh['dp'=8,'tensor'=4] {'dp','tensor'}, use_global_device_ids=true, to_apply=%region_32.33 | all-reduce | flops 1536 | bytes 12288 | tf_op jit(solution)/shard_map/psum | solution.py:324
  596.3 86.3 %all-reduce.14.cloned.1.call-done = (f32[256,256]{1,0:T(8,128)}, f32[256,256]{1,0:T(8,128)}, f32[256,256]{1,0:T(8,128)}, f32[256,256]{1,0:T(8,128)}, f32[256,102...) async-done(((f32[256,256]{1,0:T(8,128)}, f32[256,256]{1,0:T(8,128)}, f32[256,256]{1,0:T(8,128)}, f32[256,256]{1,0:T(8,128)}, f32[256,1024]{1,0:T(8,128)}, ...) | async-done | bytes 3670032 | tf_op jit(solution)/shard_map/psum | solution.py:324
  (398 shorter events, 229.3 us)
Async XLA Ops:
  7.2 99.4 %copy-start = (bf16[256,1024]{1,0:T(8,128)(2,1)S(1)}, bf16[256,1024]{1,0:T(8,128)(2,1)}, u32[]{:S(2)}) copy-start(bf16[256,1024]{1,0:T(8,128)(2,1)} %param.35) | copy-start | bytes 1572868
  7.2 209.2 %all-reduce.10.cloned.1.call-start = ((), (), s32[]{:S(2)}) async-start(), calls=%async_computation | async-start | bytes 2097152 | tf_op jit(solution)/shard_map/psum | solution.py:230
  13.9 102.4 %copy-start.34 = (f32[256,16]{1,0:T(8,128)}, f32[256,16]{1,0:T(8,128)S(1)}, u32[]{:S(2)}) copy-start(f32[256,16]{1,0:T(8,128)S(1)} %convert_divide_fusion) | copy-start | bytes 49156
  119.6 25.2 %copy-start.90 = (f32[512]{0:T(512)S(1)}, f32[512]{0:T(512)}, u32[]{:S(2)}) copy-start(f32[512]{0:T(512)} %param.38) | copy-start | bytes 6148
  119.9 12.3 %collective-permute-start = (bf16[256,512]{1,0:T(8,128)(2,1)S(1)}, bf16[256,512]{1,0:T(8,128)(2,1)S(1)}, u32[]{:S(2)}, u32[]{:S(2)}) collective-permute-start(bf16[256,512]{1,0:T(8,128)(2,1)S(1)} %convolution_convert_fusion.11), channel_id=1, source_target_pairs={{0,1},{1,2},{2,3},{3,0},{4,5},{5,6},{6,7},{7,4},{8,9},{9,10},{10,1... | collective-permute-start | bytes 786440 | tf_op jit(solution)/shard_map/ppermute | solution.py:26
  123.0 13.5 %collective-permute-start.2 = (bf16[256,512]{1,0:T(8,128)(2,1)S(1)}, bf16[256,512]{1,0:T(8,128)(2,1)S(1)}, u32[]{:S(2)}, u32[]{:S(2)}) collective-permute-start(bf16[256,512]{1,0:T(8,128)(2,1)S(1)} %convolution_convert_fusion.11), channel_id=1, source_target_pairs={{1,0},{2,1},{3,2},{0,3},{5,4},{6,5},{7,6},{4,7},{9,8},{10,9},{11,1... | collective-permute-start | bytes 786440 | tf_op jit(solution)/shard_map/ppermute | solution.py:28
  132.2 10.4 %collective-permute-start.1 = (bf16[256,512]{1,0:T(8,128)(2,1)S(1)}, bf16[256,512]{1,0:T(8,128)(2,1)S(1)}, u32[]{:S(2)}, u32[]{:S(2)}) collective-permute-start(bf16[256,512]{1,0:T(8,128)(2,1)S(1)} %collective-permute-done), channel_id=1, source_target_pairs={{0,1},{1,2},{2,3},{3,0},{4,5},{5,6},{6,7},{7,4},{8,9},{9,10},{10,1... | collective-permute-start | bytes 786440 | tf_op jit(solution)/shard_map/ppermute | solution.py:26
  160.5 56.0 %copy-start.85 = (f32[2,2,512]{2,1,0:T(2,128)}, f32[2,2,512]{2,1,0:T(2,128)S(1)}, u32[]{:S(2)}) copy-start(f32[2,2,512]{2,1,0:T(2,128)S(1)} %get-tuple-element.475) | copy-start | bytes 24580
  160.5 57.7 %copy-start.15 = (bf16[1024,2,64]{0,2,1:T(8,128)(2,1)}, bf16[1024,2,64]{0,2,1:T(8,128)(2,1)S(1)}, u32[]{:S(2)}) copy-start(bf16[1024,2,64]{0,2,1:T(8,128)(2,1)S(1)} %get-tuple-element.568) | copy-start | bytes 786436
  160.5 57.7 %copy-start.17 = (bf16[1024,2,64]{0,2,1:T(8,128)(2,1)}, bf16[1024,2,64]{0,2,1:T(8,128)(2,1)S(1)}, u32[]{:S(2)}) copy-start(bf16[1024,2,64]{0,2,1:T(8,128)(2,1)S(1)} %get-tuple-element.569) | copy-start | bytes 786436
  165.1 113.2 %all-reduce.12.cloned.1.call-start = ((), (), s32[]{:S(2)}) async-start(), calls=%async_computation.1 | async-start | bytes 2097152 | tf_op jit(solution)/shard_map/psum | solution.py:249
  226.9 175.0 %all-reduce.18.cloned.1.call-start = ((), (), s32[]{:S(2)}) async-start(), calls=%async_computation.4 | async-start | bytes 4194304 | tf_op jit(solution)/shard_map/psum | solution.py:238
  288.0 25.9 %copy-start.62 = (bf16[512,128]{1,0:T(8,128)(2,1)S(1)}, bf16[512,128]{1,0:T(8,128)(2,1)}, u32[]{:S(2)}) copy-start(bf16[512,128]{1,0:T(8,128)(2,1)} %param.40) | copy-start | bytes 393220
  316.4 279.9 %all-reduce.16.cloned.1.call-start = ((), (), s32[]{:S(2)}) async-start(), calls=%async_computation.3 | async-start | bytes 6291456 | tf_op jit(solution)/shard_map/psum | solution.py:321
  323.7 78.3 %copy-start.82 = (f32[1,2,4,128]{3,1,2,0:T(2,128)S(1)}, f32[1,2,4,128]{3,1,2,0:T(2,128)}, u32[]{:S(2)}) copy-start(f32[1,2,4,128]{3,1,2,0:T(2,128)} %copy-done.81) | copy-start | bytes 12292
  323.7 78.3 %copy-start.84 = (f32[1024]{0:T(1024)S(1)}, f32[1024]{0:T(1024)}, u32[]{:S(2)}) copy-start(f32[1024]{0:T(1024)} %copy-done.83) | copy-start | bytes 12292
  326.1 78.9 %copy-start.89 = (f32[1,2,4,128]{3,1,2,0:T(2,128)S(1)}, f32[1,2,4,128]{3,1,2,0:T(2,128)}, u32[]{:S(2)}) copy-start(f32[1,2,4,128]{3,1,2,0:T(2,128)} %copy-done.88) | copy-start | bytes 12292
  327.1 81.4 %copy-start.37 = (bf16[256,512]{1,0:T(8,128)(2,1)S(1)}, bf16[256,512]{1,0:T(8,128)(2,1)}, u32[]{:S(2)}) copy-start(bf16[256,512]{1,0:T(8,128)(2,1)} %param.37) | copy-start | bytes 786436
  327.1 355.4 %all-reduce.14.cloned.1.call-start = ((), (), s32[]{:S(2)}) async-start(), calls=%async_computation.2 | async-start | bytes 7340032 | tf_op jit(solution)/shard_map/psum | solution.py:324
  410.6 15.5 %copy-start.23 = (bf16[4096,256]{1,0:T(8,128)(2,1)}, bf16[4096,256]{1,0:T(8,128)(2,1)S(1)}, u32[]{:S(2)}) copy-start(bf16[4096,256]{1,0:T(8,128)(2,1)S(1)} %fusion.62) | copy-start | bytes 6291460
  410.6 15.5 %copy-start.4 = (f32[4096,256]{1,0:T(8,128)S(1)}, f32[4096,256]{1,0:T(8,128)}, u32[]{:S(2)}) copy-start(f32[4096,256]{1,0:T(8,128)} %copy-done.3) | copy-start | bytes 12582916
  410.6 15.5 %copy-start.74 = (f32[4096]{0:T(1024)S(1)}, f32[4096]{0:T(1024)}, u32[]{:S(2)}) copy-start(f32[4096]{0:T(1024)} %copy-done.73) | copy-start | bytes 49156
  596.3 97.4 %copy-start.70 = (f32[512,128]{1,0:T(8,128)S(1)}, f32[512,128]{1,0:T(8,128)}, u32[]{:S(2)}) copy-start(f32[512,128]{1,0:T(8,128)} %get-tuple-element.527) | copy-start | bytes 786436
  596.3 98.1 %copy-start.69 = (f32[512,128]{1,0:T(8,128)S(1)}, f32[512,128]{1,0:T(8,128)}, u32[]{:S(2)}) copy-start(f32[512,128]{1,0:T(8,128)} %get-tuple-element.528) | copy-start | bytes 786436
  (95 other events, 457.1 us)
Sparse Core Ops, SparseCore 0:
  165.2 51.2 all-reduce.9
  227.1 51.1 all-reduce.11
  316.5 85.4 all-reduce.17
  407.0 69.0 all-reduce.15
  539.7 142.8 all-reduce.13
